TPU v7x, 256 devices: a whole 4x4x8 slice. The times are simulated.
256 devices in a mesh: row: 32 (over z, y_lo, core), col: 8 (over y_hi, x).
Axes of the slice: x: 4, y: 4 (y_hi: 2, y_lo: 2; y = y_hi * 2 + y_lo), z: 8, core: 2. Of those that a mesh axis runs over, the one named last changes fastest.
Arguments:
- queries: bfloat16 [256, 256, 2240], P('row', 'col'), may hold values from -6 to 6
- keys: bfloat16 [256, 256, 2240], P('row', 'col'), may hold values from -120 to 120
- values: bfloat16 [256, 256, 2240], P('row', 'col'), may hold values from -10 to 10
- features: bfloat16 [256, 256, 11200], P('row', 'col'), may hold values from -6 to 6
- conv_weight: bfloat16 [3, 3, 11200], replicated, may hold values from -2 to 2
- conv_bias: bfloat16 [11200], replicated, may hold values from -3 to 3
Outputs:
- attended: bfloat16 [256, 256, 2240], P('row', 'col')
- gated: bfloat16 [256, 256, 5600], P('row', 'col')
All inputs are finite; a program needn't handle non-finite values.
Results may differ from a plain program's by a relative error of at most 0.001.
Values may be sent and summed in bfloat16 or wider, within the bound.
A program may use at most 128 MiB of HBM per device.

v0:
```python
import jax
import jax.numpy as jnp
from jax import lax
from jax.sharding import PartitionSpec as P

HEADS = 70
HEAD_DIM = 32
HID = 5600


def padded_2(block, sides, width):
    for axis, dim in sides:
        count = lax.axis_size(axis)
        forward = [(i, i + 1) for i in range(count - 1)]
        backward = [(target, source) for source, target in forward]
        low = lax.ppermute(
            lax.slice_in_dim(block, block.shape[dim] - width, None, axis=dim), axis, forward
        )
        high = lax.ppermute(lax.slice_in_dim(block, 0, width, axis=dim), axis, backward)
        block = jnp.concatenate([low, block, high], axis=dim)
    return block


def on_device(queries, keys, values, features, conv_weight, conv_bias):
    tile_rows, tile_cols, channels = queries.shape
    key_heads = jnp.maximum(keys.reshape(-1, HEADS, HEAD_DIM), 0)
    value_heads = values.reshape(-1, HEADS, HEAD_DIM)
    local_state = jnp.einsum(
        "thj,thi->jhi", value_heads, key_heads, preferred_element_type=jnp.float32
    ).reshape(HEAD_DIM, channels)
    local_keys = jnp.sum(key_heads, axis=0, dtype=jnp.float32).reshape(1, channels)
    state_sum, key_sum = lax.psum((local_state, local_keys), ("row", "col"))
    kv_state = state_sum.reshape(HEAD_DIM, HEADS, HEAD_DIM)
    key_total = key_sum.reshape(HEADS, HEAD_DIM)
    query_heads = jnp.maximum(queries.reshape(-1, HEADS, HEAD_DIM), 0).astype(jnp.float32)
    numerator = jnp.einsum("thi,jhi->thj", query_heads, kv_state, precision=lax.Precision.HIGHEST)
    denominator = jnp.einsum("thi,hi->th", query_heads, key_total, precision=lax.Precision.HIGHEST)
    attended = (
        (numerator / (denominator[:, :, None] + 1e-15))
        .astype(jnp.bfloat16)
        .reshape(tile_rows, tile_cols, channels)
    )
    padded = padded_2(features, (("row", 0), ("col", 1)), 1)
    weight_float = conv_weight.astype(jnp.float32)
    conv_sum = conv_bias.astype(jnp.float32)
    for tap_row in range(3):
        for tap_col in range(3):
            window = padded[tap_row : tap_row + tile_rows, tap_col : tap_col + tile_cols]
            conv_sum = conv_sum + weight_float[tap_row, tap_col] * window.astype(jnp.float32)
    gated = (conv_sum[:, :, :HID] * jax.nn.silu(conv_sum[:, :, HID:])).astype(jnp.bfloat16)
    return (attended, gated)


def solution(mesh):
    return jax.shard_map(
        on_device,
        mesh=mesh,
        in_specs=(
            P("row", "col", None),
            P("row", "col", None),
            P("row", "col", None),
            P("row", "col", None),
            P(),
            P(),
        ),
        out_specs=(P("row", "col", None), P("row", "col", None)),
        check_vma=False,
    )
```

profile of v0, /device:TPU:6, one launch (start us, length us, event | category | flops | bytes accessed | tf_op | source)
XLA Modules:
  0.0 376.9 jit_solution(7483596677770068258)
XLA Ops:
  7.2 0.0 copy-start.6
  7.2 0.0 all-reduce.2.cloned.1.call-start
  7.2 2.4 fusion.13
  9.6 2.6 collective-permute-start
  12.2 1.3 collective-permute-start.1
  13.5 1.4 broadcast_maximum_fusion.1
  14.8 5.0 %reshape.43 = bf16[256,70,32]{2,1,0:T(8,128)(2,1)} reshape(bf16[8,32,2240]{2,1,0:T(8,128)(2,1)S(1)} %broadcast_maximum_fusion.1) | data formatting | bytes 2293760 | tf_op jit(solution)/shard_map/max | solution.py:26
  19.9 4.9 %reshape.44 = bf16[256,70,32]{2,1,0:T(8,128)(2,1)} reshape(bf16[8,32,2240]{2,1,0:T(8,128)(2,1)S(1)} %copy-done.6) | data formatting | bytes 2293760 | tf_op jit(solution)/shard_map/reshape | solution.py:27
  24.8 6.3 %fusion.5 = f32[32,70,32]{0,2,1:T(8,128)} fusion(bf16[256,70,32]{2,1,0:T(8,128)(2,1)} %reshape.44, bf16[256,70,32]{2,1,0:T(8,128)(2,1)} %reshape.43), kind=kOutput, calls=%fused_computation.13 | convolution fusion | flops 36700160 | bytes 2580480 | tf_op jit(solution)/shard_map/thj,thi->jhi/dot_general | solution.py:28
  31.1 0.0 all-reduce.2.cloned.1.call-update
  31.2 1.0 fusion.14
  32.1 0.0 copy-done.5
  32.1 0.1 broadcast_maximum_fusion
  32.2 0.0 copy-start.15
  32.2 8.3 %copy.31 = bf16[8,32,11200]{2,0,1:T(8,128)(2,1)} copy(bf16[8,32,11200]{2,1,0:T(8,128)(2,1)} %param.9) | data formatting | bytes 11468800 | tf_op args[3]
  40.5 0.0 copy-done.15
  40.5 0.0 copy-start.2
  40.5 4.9 %reshape.45 = bf16[256,70,32]{2,1,0:T(8,128)(2,1)} reshape(bf16[8,32,2240]{2,1,0:T(8,128)(2,1)S(1)} %broadcast_maximum_fusion) | data formatting | bytes 2293760 | tf_op jit(solution)/shard_map/max | solution.py:35
  45.4 6.1 %copy.45 = bf16[256,70,32]{0,2,1:T(8,128)(2,1)S(1)} copy(bf16[256,70,32]{2,1,0:T(8,128)(2,1)} %reshape.45) | data formatting | bytes 2293760 | tf_op jit(solution)/shard_map/max | solution.py:35
  51.5 0.3 convert_reduce_fusion
  51.8 0.1 reshape.37
  51.9 81.2 %psum.15 = f32[70,32]{1,0:T(8,128)S(1)} all-reduce(f32[70,32]{1,0:T(8,128)S(1)} %reshape.37), channel_id=1, replica_groups=mesh['row'=32,'col'=8] {'row','col'}, use_global_device_ids=true, to_apply=%region_2.0 | all-reduce | flops 2240 | bytes 17920 | tf_op jit(solution)/shard_map/psum | solution.py:32
  133.1 0.6 fusion.11
  133.7 0.6 fusion.10
  134.3 0.0 collective-permute-done
  134.3 2.2 copy.30
  136.6 0.0 collective-permute-done.1
  136.6 2.3 copy.32
  138.9 0.0 copy-start
  138.9 1.1 copy-done
  140.0 2.1 pad_maximum_fusion.5
  142.1 5.5 %collective-permute-start.2 = (bf16[10,1,11200]{2,0,1:T(8,128)(2,1)}, bf16[10,1,11200]{2,0,1:T(8,128)(2,1)}, u32[]{:S(2)}, u32[]{:S(2)}) collective-permute-start(bf16[10,1,11200]{2,0,1:T(8,128)(2,1)} %get-tuple-element.12), channel_id=1, source_target_pairs={{0,1},{1,2},{2,3},{3,4},{4,5},{5,6},{6,7},{8,9},{9,10},{10,11},{11... | collective-permute-start | bytes 672008 | tf_op jit(solution)/shard_map/ppermute | solution.py:16
  147.6 1.9 collective-permute-start.3
  149.6 145.6 %all-reduce.2.cloned.1.call-done = f32[32,70,32]{0,2,1:T(8,128)} async-done(((f32[32,70,32]{0,2,1:T(8,128)}), f32[32,70,32]{0,2,1:T(8,128)}) %all-reduce.2.cloned.1.call-update) | async-done | bytes 286736 | tf_op jit(solution)/shard_map/psum | solution.py:32
  295.2 0.0 copy-done.4
  295.2 3.4 fusion.4
  298.6 6.0 %reshape.38 = bf16[8,32,2240]{1,0,2:T(8,128)(2,1)} reshape(bf16[256,70,32]{0,2,1:T(8,128)(2,1)} %fusion.4) | data formatting | bytes 2293760 | tf_op jit(solution)/shard_map/reshape | solution.py:41
  304.7 6.3 %copy.38 = bf16[8,32,2240]{2,1,0:T(8,128)(2,1)} copy(bf16[8,32,2240]{1,0,2:T(8,128)(2,1)} %reshape.38) | data formatting | bytes 2293760
  311.0 0.0 copy-start.10
  311.0 0.0 copy-start.11
  311.0 0.0 copy-start.12
  311.0 0.0 copy-start.13
  311.1 0.0 collective-permute-done.2
  311.1 0.0 collective-permute-done.3
  311.1 22.1 %maximum_maximum_fusion = (bf16[10,33,11200]{2,0,1:T(8,128)(2,1)}, bf16[10,33,11200]{2,0,1:T(8,128)(2,1)}) fusion(bf16[1,32,11200]{2,0,1:T(2,128)(2,1)} %copy-done, bf16[8,32,11200]{2,0,1:T(8,128)(2,1)} %copy.31, bf16[1,32,11200]{2,0,1:T(2,128)(2,1)S(1)} %copy.30, bf16[10,1,11200]{2,0,1:T(8,128)(2,1)} %collective-permute-done.2, ...), kind=kLoop, calls=%fused_computation | loop fusion | flops 59136000 | bytes 22400000 | tf_op jit(solution)/shard_map/concatenate | solution.py:20
  333.3 29.1 %multiply_add_fusion = f32[8,32,11200]{2,0,1:T(8,128)} fusion(bf16[8,32,11200]{2,0,1:T(8,128)(2,1)S(1)} %bitcast.28, bf16[10,33,11200]{2,0,1:T(8,128)(2,1)} %get-tuple-element.11, bf16[1,32,11200]{2,0,1:T(2,128)(2,1)S(1)} %copy-done.1, bf16[10,33,11200]{2,0,1:T(8,128)(2,1)} %get-tuple-element.10, bf16[1,32,11200]{2,0,1:T(2,128)(2,1)S(1)} %copy.30, ...), kind=kLoop, calls=%fused_computation.2 | loop fusion | flops 94617600 | bytes 53491200 | tf_op jit(solution)/shard_map/add | solution.py:49
  362.4 5.2 %fusion = bf16[8,32,5600]{2,0,1:T(8,128)(2,1)S(1)} fusion(f32[8,32,11200]{2,0,1:T(8,128)} %multiply_add_fusion), kind=kLoop, calls=%fused_computation.4 | loop fusion | flops 8601600 | bytes 14336000 | tf_op jit(solution)/shard_map/convert_element_type | solution.py:50
  367.7 2.4 copy.39
  (26 shorter events, 0.1 us)
Async XLA Ops:
  7.2 12.7 %copy-start.6 = (bf16[8,32,2240]{2,1,0:T(8,128)(2,1)S(1)}, bf16[8,32,2240]{2,1,0:T(8,128)(2,1)}, u32[]{:S(2)}) copy-start(bf16[8,32,2240]{2,1,0:T(8,128)(2,1)} %param.8) | copy-start | bytes 3440644
  7.2 288.0 %all-reduce.2.cloned.1.call-start = ((), (), s32[]{:S(2)}) async-start(), calls=%async_computation | async-start | bytes 2293760 | tf_op jit(solution)/shard_map/psum | solution.py:32
  9.6 124.7 %collective-permute-start = (bf16[1,32,11200]{2,1,0:T(8,128)(2,1)S(1)}, bf16[1,32,11200]{2,1,0:T(8,128)(2,1)}, u32[]{:S(2)}, u32[]{:S(2)}) collective-permute-start(bf16[1,32,11200]{2,1,0:T(8,128)(2,1)S(1)} %get-tuple-element.14), channel_id=1, source_target_pairs={{0,8},{8,16},{16,24},{24,32},{32,40},{40,48},{48,56},{56,64},{64,7... | collective-permute-start | bytes 2150408 | tf_op jit(solution)/shard_map/ppermute | solution.py:16
  12.2 124.4 %collective-permute-start.1 = (bf16[1,32,11200]{2,1,0:T(8,128)(2,1)}, bf16[1,32,11200]{2,1,0:T(8,128)(2,1)}, u32[]{:S(2)}, u32[]{:S(2)}) collective-permute-start(bf16[1,32,11200]{2,1,0:T(8,128)(2,1)} %get-tuple-element.15), channel_id=1, source_target_pairs={{8,0},{16,8},{24,16},{32,24},{40,32},{48,40},{56,48},{64,56},{72,6... | collective-permute-start | bytes 2150408 | tf_op jit(solution)/shard_map/ppermute | solution.py:19
  24.8 6.4 %copy-start.7 = (bf16[3,3,11200]{2,1,0:T(4,128)(2,1)S(1)}, bf16[3,3,11200]{2,1,0:T(4,128)(2,1)}, u32[]{:S(2)}) copy-start(bf16[3,3,11200]{2,1,0:T(4,128)(2,1)} %param.10) | copy-start | bytes 604804
  24.8 7.3 %copy-start.5 = (bf16[8,32,2240]{2,1,0:T(8,128)(2,1)S(1)}, bf16[8,32,2240]{2,1,0:T(8,128)(2,1)}, u32[]{:S(2)}) copy-start(bf16[8,32,2240]{2,1,0:T(8,128)(2,1)} %param.6) | copy-start | bytes 3440644
  32.2 8.3 %copy-start.15 = (bf16[11200]{0:T(1024)(128)(2,1)S(1)}, bf16[11200]{0:T(1024)(128)(2,1)}, u32[]{:S(2)}) copy-start(bf16[11200]{0:T(1024)(128)(2,1)} %param.11) | copy-start | bytes 67204
  40.5 11.0 %copy-start.2 = (bf16[8,32,2240]{2,1,0:T(8,128)(2,1)S(1)}, bf16[8,32,2240]{2,1,0:T(8,128)(2,1)}, u32[]{:S(2)}) copy-start(bf16[8,32,2240]{2,1,0:T(8,128)(2,1)} %param.7) | copy-start | bytes 3440644
  51.5 82.8 %copy-start.3 = (bf16[256,70,32]{0,2,1:T(8,128)(2,1)}, bf16[256,70,32]{0,2,1:T(8,128)(2,1)S(1)}, u32[]{:S(2)}) copy-start(bf16[256,70,32]{0,2,1:T(8,128)(2,1)S(1)} %copy.45) | copy-start | bytes 3440644
  136.5 158.7 %copy-start.4 = (bf16[256,70,32]{0,2,1:T(8,128)(2,1)S(1)}, bf16[256,70,32]{0,2,1:T(8,128)(2,1)}, u32[]{:S(2)}) copy-start(bf16[256,70,32]{0,2,1:T(8,128)(2,1)} %copy-done.3) | copy-start | bytes 3440644
  136.5 158.7 %copy-start.14 = (f32[256,70]{0,1:T(8,128)S(1)}, f32[256,70]{0,1:T(8,128)}, u32[]{:S(2)}) copy-start(f32[256,70]{0,1:T(8,128)} %fusion.10) | copy-start | bytes 215044
  138.9 1.1 copy-start
  142.1 169.0 %collective-permute-start.2 = (bf16[10,1,11200]{2,0,1:T(8,128)(2,1)}, bf16[10,1,11200]{2,0,1:T(8,128)(2,1)}, u32[]{:S(2)}, u32[]{:S(2)}) collective-permute-start(bf16[10,1,11200]{2,0,1:T(8,128)(2,1)} %get-tuple-element.12), channel_id=1, source_target_pairs={{0,1},{1,2},{2,3},{3,4},{4,5},{5,6},{6,7},{8,9},{9,10},{10,11},{11... | collective-permute-start | bytes 672008 | tf_op jit(solution)/shard_map/ppermute | solution.py:16
  147.6 163.4 %collective-permute-start.3 = (bf16[10,1,11200]{2,0,1:T(8,128)(2,1)S(1)}, bf16[10,1,11200]{2,0,1:T(8,128)(2,1)}, u32[]{:S(2)}, u32[]{:S(2)}) collective-permute-start(bf16[10,1,11200]{2,0,1:T(8,128)(2,1)S(1)} %get-tuple-element.13), channel_id=1, source_target_pairs={{1,0},{2,1},{3,2},{4,3},{5,4},{6,5},{7,6},{9,8},{10,9},{11,10},{12... | collective-permute-start | bytes 672008 | tf_op jit(solution)/shard_map/ppermute | solution.py:19
  304.7 28.5 %slice-start = ((s8[5767168]{0:T(1024)(128)(4,1)}), s8[1572864]{0:T(1024)(128)(4,1)S(1)}, s32[]{:S(2)}) async-start(s8[5767168]{0:T(1024)(128)(4,1)} %bitcast.27), calls=%async_computation.1 | async-start | bytes 3145728
  311.0 22.2 %slice-start.1 = ((s8[5767168]{0:T(1024)(128)(4,1)}), s8[4194304]{0:T(1024)(128)(4,1)S(1)}, s32[]{:S(2)}) async-start(s8[5767168]{0:T(1024)(128)(4,1)} %bitcast.27), calls=%async_computation.2 | async-start | bytes 8388608
  311.0 22.2 %copy-start.1 = (bf16[1,32,11200]{2,0,1:T(2,128)(2,1)S(1)}, bf16[1,32,11200]{2,0,1:T(2,128)(2,1)}, u32[]{:S(2)}) copy-start(bf16[1,32,11200]{2,0,1:T(2,128)(2,1)} %copy-done) | copy-start | bytes 2150404
  311.0 22.2 %copy-start.8 = (f32[1,1,11200]{2,1,0:T(1,128)S(1)}, f32[1,1,11200]{2,1,0:T(1,128)}, u32[]{:S(2)}) copy-start(f32[1,1,11200]{2,1,0:T(1,128)} %get-tuple-element.19) | copy-start | bytes 134404
  311.0 22.2 %copy-start.9 = (f32[1,1,11200]{2,1,0:T(1,128)S(1)}, f32[1,1,11200]{2,1,0:T(1,128)}, u32[]{:S(2)}) copy-start(f32[1,1,11200]{2,1,0:T(1,128)} %get-tuple-element.20) | copy-start | bytes 134404
  311.0 22.2 %copy-start.10 = (f32[1,1,11200]{2,1,0:T(1,128)S(1)}, f32[1,1,11200]{2,1,0:T(1,128)}, u32[]{:S(2)}) copy-start(f32[1,1,11200]{2,1,0:T(1,128)} %get-tuple-element.21) | copy-start | bytes 134404
  311.0 22.2 %copy-start.11 = (f32[1,1,11200]{2,1,0:T(1,128)S(1)}, f32[1,1,11200]{2,1,0:T(1,128)}, u32[]{:S(2)}) copy-start(f32[1,1,11200]{2,1,0:T(1,128)} %get-tuple-element.22) | copy-start | bytes 134404
  311.0 22.2 %copy-start.12 = (f32[1,1,11200]{2,1,0:T(1,128)S(1)}, f32[1,1,11200]{2,1,0:T(1,128)}, u32[]{:S(2)}) copy-start(f32[1,1,11200]{2,1,0:T(1,128)} %get-tuple-element.23) | copy-start | bytes 134404
  311.0 22.2 %copy-start.13 = (f32[1,1,11200]{2,1,0:T(1,128)S(1)}, f32[1,1,11200]{2,1,0:T(1,128)}, u32[]{:S(2)}) copy-start(f32[1,1,11200]{2,1,0:T(1,128)} %get-tuple-element.24) | copy-start | bytes 134404
Sparse Core Ops, SparseCore 0:
  31.3 263.8 all-reduce.1
where the time goes:
time: 378 us; the launch traced here: 377 us
  waiting for transfers between devices  146 us (39%)
  blocking collectives  81.2 us (21%)
  other arithmetic  60.9 us (16%)
  local copies, waits for them, and re-layouts  53.1 us (14%)
  between operations  14.3 us (4%)
  starting transfers between devices  11.4 us (3%)
  matrix products  10.4 us (3%)
    psum x1, waiting for transfers between devices, on_device(): state_sum, key_sum = lax.psum((local_state, local_keys), ('row', 'col'))  146 us
    psum x1, blocking collectives, on_device(): state_sum, key_sum = lax.psum((local_state, local_keys), ('row', 'col'))  81.2 us
    add x1, other arithmetic, on_device(): conv_sum + weight_float[tap_row, tap_col] * window.astype(jnp.float32)  29.1 us
    concatenate x1, other arithmetic, padded_2(): block = jnp.concatenate([low, block, high], axis=dim)  22.1 us
    unnamed x39, local copies, waits for them, and re-layouts  18.2 us
    max x2, local copies, waits for them, and re-layouts, on_device(): jnp.maximum(queries.reshape(-1, HEADS, HEAD_DIM), 0).astype(jnp.float32)  11 us
    ppermute x2, starting transfers between devices, padded_2(): lax.ppermute(lax.slice_in_dim(block, block.shape[dim] - width, None, axis...  8.14 us
  transfers between devices with their start and end apart: 5, of which 1 were waited for; matrix products, arithmetic and copies ran while one was open for 16% of the time, Pallas kernels for 0%

commit v1 on v0

--- a/solution.py
+++ b/solution.py
@@ -29,7 +29,7 @@
         "thj,thi->jhi", value_heads, key_heads, preferred_element_type=jnp.float32
     ).reshape(HEAD_DIM, channels)
     local_keys = jnp.sum(key_heads, axis=0, dtype=jnp.float32).reshape(1, channels)
-    state_sum, key_sum = lax.psum((local_state, local_keys), ("row", "col"))
+    state_sum, key_sum = lax.psum(lax.psum((local_state, local_keys), "row"), "col")
     kv_state = state_sum.reshape(HEAD_DIM, HEADS, HEAD_DIM)
     key_total = key_sum.reshape(HEADS, HEAD_DIM)
     query_heads = jnp.maximum(queries.reshape(-1, HEADS, HEAD_DIM), 0).astype(jnp.float32)

time: 378 us -> 424 us (1.12)
  waiting for transfers between devices: 146 us -> 170 us
  blocking collectives: 81.2 us -> 99.7 us
    psum x1 -> x2, waiting for transfers between devices: 146 us -> 170 us  [the longest x1 91.5 us: on_device(): lax.psum((local_state, local_keys), 'row')]
    psum x1 -> x2, blocking collectives: 81.2 us -> 99.7 us  [the longest x1 63 us: on_device(): lax.psum((local_state, local_keys), 'row')]
    unnamed x39 -> x37, local copies, waits for them, and re-layouts: 18.2 us -> 18.2 us
  transfers between devices with their start and end apart: 5 -> 6, of which waited for: 1 -> 2; matrix products, arithmetic and copies ran while one was open for 16% -> 15% of each run, Pallas kernels for 0% -> 0%
where the time goes in v1:
time: 424 us; the launch traced here: 422 us
  waiting for transfers between devices  170 us (40%)
  blocking collectives  99.7 us (24%)
  other arithmetic  60.2 us (14%)
  local copies, waits for them, and re-layouts  56.8 us (13%)
  between operations  14.4 us (3%)
  starting transfers between devices  10.8 us (3%)
  matrix products  9.28 us (2%)
    psum x1, waiting for transfers between devices, on_device(): lax.psum((local_state, local_keys), 'row')  91.5 us
    psum x1, waiting for transfers between devices, on_device(): lax.psum(lax.psum((local_state, local_keys), 'row'), 'col')  79 us
    psum x1, blocking collectives, on_device(): lax.psum((local_state, local_keys), 'row')  63 us
    psum x1, blocking collectives, on_device(): lax.psum(lax.psum((local_state, local_keys), 'row'), 'col')  36.7 us
    add x1, other arithmetic, on_device(): conv_sum + weight_float[tap_row, tap_col] * window.astype(jnp.float32)  29 us
    concatenate x1, other arithmetic, padded_2(): block = jnp.concatenate([low, block, high], axis=dim)  22.2 us
    unnamed x37, local copies, waits for them, and re-layouts  18.2 us
    max x2, local copies, waits for them, and re-layouts, on_device(): jnp.maximum(queries.reshape(-1, HEADS, HEAD_DIM), 0).astype(jnp.float32)  11 us
  transfers between devices with their start and end apart: 6, of which 2 were waited for; matrix products, arithmetic and copies ran while one was open for 15% of the time, Pallas kernels for 0%

profile of v1, /device:TPU:6, one launch (start us, length us, event | category | flops | bytes accessed | tf_op | source)
XLA Modules:
  0.0 421.6 jit_solution(331611903508125354)
XLA Ops:
  7.2 0.0 all-reduce.3.cloned.1.call-start
  7.2 2.4 fusion.8
  9.6 2.6 collective-permute-start
  12.2 1.3 collective-permute-start.1
  13.5 1.4 broadcast_maximum_fusion.1
  14.9 5.0 %reshape.41 = bf16[256,70,32]{2,1,0:T(8,128)(2,1)} reshape(bf16[8,32,2240]{2,1,0:T(8,128)(2,1)S(1)} %broadcast_maximum_fusion.1) | data formatting | bytes 2293760 | tf_op jit(solution)/shard_map/max | solution.py:26
  19.9 4.9 %reshape.42 = bf16[256,70,32]{2,1,0:T(8,128)(2,1)} reshape(bf16[8,32,2240]{2,1,0:T(8,128)(2,1)S(1)} %copy-done.6) | data formatting | bytes 2293760 | tf_op jit(solution)/shard_map/reshape | solution.py:27
  24.8 5.3 %fusion.1 = f32[70,32,32]{2,1,0:T(8,128)S(1)} fusion(bf16[256,70,32]{2,1,0:T(8,128)(2,1)} %reshape.42, bf16[256,70,32]{2,1,0:T(8,128)(2,1)} %reshape.41), kind=kOutput, calls=%fused_computation.7 | convolution fusion | flops 36700160 | bytes 2580480 | tf_op jit(solution)/shard_map/thj,thi->jhi/dot_general | solution.py:28
  30.2 1.1 copy.33
  31.2 0.0 all-reduce.3.cloned.1.call-update
  31.2 0.0 all-reduce.5.cloned.1.call-start
  31.3 1.0 fusion.9
  32.3 0.1 broadcast_maximum_fusion
  32.4 0.0 copy-start.2
  32.4 5.0 %reshape.43 = bf16[256,70,32]{2,1,0:T(8,128)(2,1)} reshape(bf16[8,32,2240]{2,1,0:T(8,128)(2,1)S(1)} %broadcast_maximum_fusion) | data formatting | bytes 2293760 | tf_op jit(solution)/shard_map/max | solution.py:35
  37.3 6.1 %copy.50 = bf16[256,70,32]{0,2,1:T(8,128)(2,1)S(1)} copy(bf16[256,70,32]{2,1,0:T(8,128)(2,1)} %reshape.43) | data formatting | bytes 2293760 | tf_op jit(solution)/shard_map/max | solution.py:35
  43.4 0.0 copy-done.2
  43.4 0.0 copy-start.3
  43.4 0.3 convert_reduce_fusion
  43.7 63.0 %psum.30 = f32[1,2240]{1,0:T(1,128)S(1)} all-reduce(f32[1,2240]{1,0:T(1,128)S(1)} %reshape.36), channel_id=1, replica_groups=mesh['row'=32,'col'=8] {'row'}, use_global_device_ids=true, to_apply=%region_3.0 | all-reduce | flops 2240 | bytes 17920 | tf_op jit(solution)/shard_map/psum | solution.py:32
  106.7 0.1 reshape.37
  106.8 36.7 %psum.31 = f32[70,32]{1,0:T(8,128)S(1)} all-reduce(f32[70,32]{1,0:T(8,128)S(1)} %reshape.37), channel_id=1, replica_groups=mesh['row'=32,'col'=8] {'col'}, use_global_device_ids=true, to_apply=%region_4.0 | all-reduce | flops 2240 | bytes 17920 | tf_op jit(solution)/shard_map/psum | solution.py:32
  143.5 0.6 fusion.6
  144.1 0.0 copy-start.14
  144.1 8.3 %copy.37 = bf16[8,32,11200]{2,0,1:T(8,128)(2,1)} copy(bf16[8,32,11200]{2,1,0:T(8,128)(2,1)} %param.9) | data formatting | bytes 11468800 | tf_op args[3]
  152.4 91.5 %all-reduce.3.cloned.1.call-done = f32[32,2240]{1,0:T(8,128)} async-done(((f32[32,2240]{1,0:T(8,128)}), f32[32,2240]{1,0:T(8,128)}) %all-reduce.3.cloned.1.call-update) | async-done | bytes 286736 | tf_op jit(solution)/shard_map/psum | solution.py:32
  243.9 1.4 reshape.35
  245.3 1.2 copy.34
  246.5 0.0 all-reduce.5.cloned.1.call-update
  246.5 0.0 collective-permute-done
  246.5 2.2 copy.36
  248.8 0.0 collective-permute-done.1
  248.8 2.3 copy.38
  251.1 0.0 copy-start
  251.1 1.1 copy-done
  252.2 2.1 pad_maximum_fusion.5
  254.3 4.9 %collective-permute-start.2 = (bf16[10,1,11200]{2,0,1:T(8,128)(2,1)}, bf16[10,1,11200]{2,0,1:T(8,128)(2,1)}, u32[]{:S(2)}, u32[]{:S(2)}) collective-permute-start(bf16[10,1,11200]{2,0,1:T(8,128)(2,1)} %get-tuple-element.12), channel_id=1, source_target_pairs={{0,1},{1,2},{2,3},{3,4},{4,5},{5,6},{6,7},{8,9},{9,10},{10,11},{11... | collective-permute-start | bytes 672008 | tf_op jit(solution)/shard_map/ppermute | solution.py:16
  259.2 1.9 collective-permute-start.3
  261.1 79.0 %all-reduce.5.cloned.1.call-done = f32[32,70,32]{2,0,1:T(8,128)} async-done(((f32[32,70,32]{2,0,1:T(8,128)}), f32[32,70,32]{2,0,1:T(8,128)}) %all-reduce.5.cloned.1.call-update) | async-done | bytes 286736 | tf_op jit(solution)/shard_map/psum | solution.py:32
  340.1 3.4 fusion.4
  343.5 6.0 %reshape.38 = bf16[8,32,2240]{1,0,2:T(8,128)(2,1)} reshape(bf16[256,70,32]{0,2,1:T(8,128)(2,1)} %fusion.4) | data formatting | bytes 2293760 | tf_op jit(solution)/shard_map/reshape | solution.py:41
  349.5 6.3 %copy.44 = bf16[8,32,2240]{2,1,0:T(8,128)(2,1)} copy(bf16[8,32,2240]{1,0,2:T(8,128)(2,1)} %reshape.38) | data formatting | bytes 2293760
  355.9 0.0 collective-permute-done.2
  355.9 0.0 collective-permute-done.3
  355.9 22.2 %maximum_maximum_fusion = (bf16[10,33,11200]{2,0,1:T(8,128)(2,1)}, bf16[10,33,11200]{2,0,1:T(8,128)(2,1)}) fusion(bf16[1,32,11200]{2,0,1:T(2,128)(2,1)} %copy-done, bf16[8,32,11200]{2,0,1:T(8,128)(2,1)} %copy.37, bf16[1,32,11200]{2,0,1:T(2,128)(2,1)S(1)} %copy.36, bf16[10,1,11200]{2,0,1:T(8,128)(2,1)} %collective-permute-done.2, ...), kind=kLoop, calls=%fused_computation | loop fusion | flops 59136000 | bytes 22400000 | tf_op jit(solution)/shard_map/concatenate | solution.py:20
  378.2 29.0 %multiply_add_fusion = f32[8,32,11200]{2,0,1:T(8,128)} fusion(bf16[8,32,11200]{2,0,1:T(8,128)(2,1)S(1)} %bitcast.29, bf16[10,33,11200]{2,0,1:T(8,128)(2,1)} %get-tuple-element.11, bf16[1,32,11200]{2,0,1:T(2,128)(2,1)S(1)} %copy-done.1, bf16[10,33,11200]{2,0,1:T(8,128)(2,1)} %get-tuple-element.10, bf16[1,32,11200]{2,0,1:T(2,128)(2,1)S(1)} %copy.36, ...), kind=kLoop, calls=%fused_computation.2 | loop fusion | flops 94617600 | bytes 53491200 | tf_op jit(solution)/shard_map/add | solution.py:49
  407.1 5.2 %fusion = bf16[8,32,5600]{2,0,1:T(8,128)(2,1)S(1)} fusion(f32[8,32,11200]{2,0,1:T(8,128)} %multiply_add_fusion), kind=kLoop, calls=%fused_computation.4 | loop fusion | flops 8601600 | bytes 14336000 | tf_op jit(solution)/shard_map/convert_element_type | solution.py:50
  412.4 2.4 copy.45
  (33 shorter events, 0.1 us)
Async XLA Ops:
  7.2 12.7 %copy-start.6 = (bf16[8,32,2240]{2,1,0:T(8,128)(2,1)S(1)}, bf16[8,32,2240]{2,1,0:T(8,128)(2,1)}, u32[]{:S(2)}) copy-start(bf16[8,32,2240]{2,1,0:T(8,128)(2,1)} %param.8) | copy-start | bytes 3440644
  7.2 236.7 %all-reduce.3.cloned.1.call-start = ((), (), s32[]{:S(2)}) async-start(), calls=%async_computation | async-start | bytes 589824 | tf_op jit(solution)/shard_map/psum | solution.py:32
  9.6 236.9 %collective-permute-start = (bf16[1,32,11200]{2,1,0:T(8,128)(2,1)S(1)}, bf16[1,32,11200]{2,1,0:T(8,128)(2,1)}, u32[]{:S(2)}, u32[]{:S(2)}) collective-permute-start(bf16[1,32,11200]{2,1,0:T(8,128)(2,1)S(1)} %get-tuple-element.14), channel_id=1, source_target_pairs={{0,8},{8,16},{16,24},{24,32},{32,40},{40,48},{48,56},{56,64},{64,7... | collective-permute-start | bytes 2150408 | tf_op jit(solution)/shard_map/ppermute | solution.py:16
  12.2 236.6 %collective-permute-start.1 = (bf16[1,32,11200]{2,1,0:T(8,128)(2,1)}, bf16[1,32,11200]{2,1,0:T(8,128)(2,1)}, u32[]{:S(2)}, u32[]{:S(2)}) collective-permute-start(bf16[1,32,11200]{2,1,0:T(8,128)(2,1)} %get-tuple-element.15), channel_id=1, source_target_pairs={{8,0},{16,8},{24,16},{32,24},{40,32},{48,40},{56,48},{64,56},{72,6... | collective-permute-start | bytes 2150408 | tf_op jit(solution)/shard_map/ppermute | solution.py:19
  24.8 6.5 %copy-start.7 = (bf16[3,3,11200]{2,1,0:T(4,128)(2,1)S(1)}, bf16[3,3,11200]{2,1,0:T(4,128)(2,1)}, u32[]{:S(2)}) copy-start(bf16[3,3,11200]{2,1,0:T(4,128)(2,1)} %param.10) | copy-start | bytes 604804
  24.8 7.4 %copy-start.5 = (bf16[8,32,2240]{2,1,0:T(8,128)(2,1)S(1)}, bf16[8,32,2240]{2,1,0:T(8,128)(2,1)}, u32[]{:S(2)}) copy-start(bf16[8,32,2240]{2,1,0:T(8,128)(2,1)} %param.6) | copy-start | bytes 3440644
  31.2 308.8 %all-reduce.5.cloned.1.call-start = ((), (), s32[]{:S(2)}) async-start(), calls=%async_computation.1 | async-start | bytes 2293760 | tf_op jit(solution)/shard_map/psum | solution.py:32
  32.4 11.0 %copy-start.2 = (bf16[8,32,2240]{2,1,0:T(8,128)(2,1)S(1)}, bf16[8,32,2240]{2,1,0:T(8,128)(2,1)}, u32[]{:S(2)}) copy-start(bf16[8,32,2240]{2,1,0:T(8,128)(2,1)} %param.7) | copy-start | bytes 3440644
  43.4 109.0 %copy-start.3 = (bf16[256,70,32]{0,2,1:T(8,128)(2,1)}, bf16[256,70,32]{0,2,1:T(8,128)(2,1)S(1)}, u32[]{:S(2)}) copy-start(bf16[256,70,32]{0,2,1:T(8,128)(2,1)S(1)} %copy.50) | copy-start | bytes 3440644
  144.1 8.3 %copy-start.14 = (bf16[11200]{0:T(1024)(128)(2,1)S(1)}, bf16[11200]{0:T(1024)(128)(2,1)}, u32[]{:S(2)}) copy-start(bf16[11200]{0:T(1024)(128)(2,1)} %param.11) | copy-start | bytes 67204
  248.8 91.3 %copy-start.4 = (bf16[256,70,32]{0,2,1:T(8,128)(2,1)S(1)}, bf16[256,70,32]{0,2,1:T(8,128)(2,1)}, u32[]{:S(2)}) copy-start(bf16[256,70,32]{0,2,1:T(8,128)(2,1)} %copy-done.3) | copy-start | bytes 3440644
  251.1 1.1 copy-start
  254.3 101.6 %collective-permute-start.2 = (bf16[10,1,11200]{2,0,1:T(8,128)(2,1)}, bf16[10,1,11200]{2,0,1:T(8,128)(2,1)}, u32[]{:S(2)}, u32[]{:S(2)}) collective-permute-start(bf16[10,1,11200]{2,0,1:T(8,128)(2,1)} %get-tuple-element.12), channel_id=1, source_target_pairs={{0,1},{1,2},{2,3},{3,4},{4,5},{5,6},{6,7},{8,9},{9,10},{10,11},{11... | collective-permute-start | bytes 672008 | tf_op jit(solution)/shard_map/ppermute | solution.py:16
  259.2 96.7 %collective-permute-start.3 = (bf16[10,1,11200]{2,0,1:T(8,128)(2,1)S(1)}, bf16[10,1,11200]{2,0,1:T(8,128)(2,1)}, u32[]{:S(2)}, u32[]{:S(2)}) collective-permute-start(bf16[10,1,11200]{2,0,1:T(8,128)(2,1)S(1)} %get-tuple-element.13), channel_id=1, source_target_pairs={{1,0},{2,1},{3,2},{4,3},{5,4},{6,5},{7,6},{9,8},{10,9},{11,10},{12... | collective-permute-start | bytes 672008 | tf_op jit(solution)/shard_map/ppermute | solution.py:19
  349.5 28.6 %slice-start = ((s8[5767168]{0:T(1024)(128)(4,1)}), s8[1572864]{0:T(1024)(128)(4,1)S(1)}, s32[]{:S(2)}) async-start(s8[5767168]{0:T(1024)(128)(4,1)} %bitcast.28), calls=%async_computation.2 | async-start | bytes 3145728
  355.8 22.2 %slice-start.1 = ((s8[5767168]{0:T(1024)(128)(4,1)}), s8[4194304]{0:T(1024)(128)(4,1)S(1)}, s32[]{:S(2)}) async-start(s8[5767168]{0:T(1024)(128)(4,1)} %bitcast.28), calls=%async_computation.3 | async-start | bytes 8388608
  355.8 22.3 %copy-start.1 = (bf16[1,32,11200]{2,0,1:T(2,128)(2,1)S(1)}, bf16[1,32,11200]{2,0,1:T(2,128)(2,1)}, u32[]{:S(2)}) copy-start(bf16[1,32,11200]{2,0,1:T(2,128)(2,1)} %copy-done) | copy-start | bytes 2150404
  355.8 22.3 %copy-start.8 = (f32[1,1,11200]{2,1,0:T(1,128)S(1)}, f32[1,1,11200]{2,1,0:T(1,128)}, u32[]{:S(2)}) copy-start(f32[1,1,11200]{2,1,0:T(1,128)} %get-tuple-element.19) | copy-start | bytes 134404
  355.8 22.3 %copy-start.9 = (f32[1,1,11200]{2,1,0:T(1,128)S(1)}, f32[1,1,11200]{2,1,0:T(1,128)}, u32[]{:S(2)}) copy-start(f32[1,1,11200]{2,1,0:T(1,128)} %get-tuple-element.20) | copy-start | bytes 134404
  355.8 22.3 %copy-start.10 = (f32[1,1,11200]{2,1,0:T(1,128)S(1)}, f32[1,1,11200]{2,1,0:T(1,128)}, u32[]{:S(2)}) copy-start(f32[1,1,11200]{2,1,0:T(1,128)} %get-tuple-element.21) | copy-start | bytes 134404
  355.8 22.3 %copy-start.11 = (f32[1,1,11200]{2,1,0:T(1,128)S(1)}, f32[1,1,11200]{2,1,0:T(1,128)}, u32[]{:S(2)}) copy-start(f32[1,1,11200]{2,1,0:T(1,128)} %get-tuple-element.22) | copy-start | bytes 134404
  355.9 22.3 %copy-start.12 = (f32[1,1,11200]{2,1,0:T(1,128)S(1)}, f32[1,1,11200]{2,1,0:T(1,128)}, u32[]{:S(2)}) copy-start(f32[1,1,11200]{2,1,0:T(1,128)} %get-tuple-element.23) | copy-start | bytes 134404
  355.9 22.3 %copy-start.13 = (f32[1,1,11200]{2,1,0:T(1,128)S(1)}, f32[1,1,11200]{2,1,0:T(1,128)}, u32[]{:S(2)}) copy-start(f32[1,1,11200]{2,1,0:T(1,128)} %get-tuple-element.24) | copy-start | bytes 134404
Sparse Core Ops, SparseCore 0:
  31.4 212.4 all-reduce.2
  247.3 92.7 all-reduce.4
